TPU v7x, 32 devices: a whole 2x2x4 slice. The times are simulated.
32 devices in a mesh: groups: 2 (over x), hid: 16 (over z, y, core).
Axes of the slice: x: 2, y: 2, z: 4, core: 2. Of those that a mesh axis runs over, the one named last changes fastest.
Arguments:
- tokens: bfloat16 [256, 8192], P(('groups', 'hid')), parts along dimension 0, may hold values from -6 to 6
- norm_gain: float32 [8192], replicated, may hold values from 0.1 to 1.9
- gate_weight: bfloat16 [8192, 16384], P(None, 'hid'), may hold values from -0.0625 to 0.0625
- up_weight: bfloat16 [8192, 16384], P(None, 'hid'), may hold values from -0.0625 to 0.0625
- down_weight: bfloat16 [16384, 8192], P('hid'), may hold values from -0.046875 to 0.046875
- clip_scale: float32 [16384], P('hid'), may hold values from 0.002 to 0.02
Outputs:
- mixed: bfloat16 [256, 8192], P(('groups', 'hid')), parts along dimension 0
There are 2 independent parts, one for each index of `groups`. A program takes and returns all parts, laid end to end along the dimension named above; an argument that names none is the same for every part. Nothing has to cross between parts.
All inputs are finite; a program needn't handle non-finite values.
Results may differ from a plain program's by a relative error of at most 0.006.
Values may be sent and summed in bfloat16 or wider, within the bound.
A program may use at most 128 MiB of HBM per device.

v0:
```python
import jax
import jax.numpy as jnp
from jax import lax
from jax.sharding import PartitionSpec as P

FF = 16384
BLOCK = 256


def hadamard(count):
    rows = jnp.arange(count, dtype=jnp.int32)[:, None]
    cols = jnp.arange(count, dtype=jnp.int32)[None, :]
    both = rows & cols
    parity = jnp.zeros((count, count), jnp.int32)
    for place in range(max(count.bit_length(), 1)):
        parity = parity + (both >> place & 1)
    return jnp.where(parity % 2 == 0, 1.0, -1.0).astype(jnp.float32)


def normalize(rows_in, norm_gain):
    values = rows_in.astype(jnp.float32)
    inverse = lax.rsqrt(jnp.mean(values * values, axis=-1, keepdims=True) + 1e-05)
    return (values * inverse * norm_gain).astype(jnp.bfloat16)


def shards(tokens, norm_gain, gate_weight, up_weight, down_weight, clip_scale):
    whole = lax.all_gather(tokens, "hid", axis=0, tiled=True)
    normed = normalize(whole, norm_gain)
    gate = jnp.dot(normed, gate_weight, preferred_element_type=jnp.float32)
    up = jnp.dot(normed, up_weight, preferred_element_type=jnp.float32)
    hidden = jax.nn.silu(gate) * up
    row_count = hidden.shape[0]
    local_blocks = hidden.shape[1] // BLOCK
    shaped = hidden.reshape(row_count, local_blocks, BLOCK)
    shaped = jnp.einsum("tbc,cd->tbd", shaped, hadamard(BLOCK), precision=lax.Precision.HIGHEST)
    gathered = lax.all_to_all(shaped, "hid", split_axis=0, concat_axis=1, tiled=True)
    table = hadamard(gathered.shape[1])
    turned = jnp.einsum("tbc,be->tec", gathered, table, precision=lax.Precision.HIGHEST)
    shaped = lax.all_to_all(
        turned.astype(jnp.bfloat16), "hid", split_axis=1, concat_axis=0, tiled=True
    ).astype(turned.dtype)
    rotated = shaped.reshape(row_count, local_blocks * BLOCK) / jnp.sqrt(jnp.float32(FF))
    limit = 127.0 * clip_scale
    clipped = jnp.clip(rotated, -limit, limit).astype(jnp.bfloat16)
    summed = lax.psum_scatter(
        jnp.dot(clipped, down_weight, preferred_element_type=jnp.float32),
        "hid",
        scatter_dimension=0,
        tiled=True,
    )
    return (tokens.astype(jnp.float32) + summed).astype(jnp.bfloat16)


def solution(mesh):
    in_specs = (
        P(("groups", "hid"), None),
        P(),
        P(None, "hid"),
        P(None, "hid"),
        P("hid", None),
        P("hid"),
    )
    out_specs = P(("groups", "hid"), None)
    return jax.shard_map(shards, mesh=mesh, in_specs=in_specs, out_specs=out_specs, check_vma=False)
```

profile of v0, /device:TPU:0, one launch (start us, length us, event | category | flops | bytes accessed | tf_op | source)
XLA Modules:
  0.0 194.7 jit_solution(14691300666669389388)
XLA Ops:
  6.5 0.0 all-gather.2.cloned.1.call-start
  6.5 0.7 all-gather.2.cloned.1.call-update
  7.3 46.5 %all-gather.2.cloned.1.call-done = bf16[128,8192]{1,0:T(8,128)(2,1)} async-done(((bf16[8,8192]{1,0:T(8,128)(2,1)}), bf16[128,8192]{1,0:T(8,128)(2,1)}) %all-gather.2.cloned.1.call-update) | async-done | bytes 2097168 | tf_op jit(solution)/shard_map/all_gather | solution.py:27
  53.7 2.1 %fusion = f32[128]{0:T(128)S(1)} fusion(bf16[128,8192]{1,0:T(8,128)(2,1)} %all-gather.2.cloned.1.call-done), kind=kLoop, calls=%fused_computation.2 | loop fusion | flops 3145600 | bytes 2097664 | tf_op jit(solution)/shard_map/reduce_sum | solution.py:22
  55.8 0.0 copy-start
  55.8 0.0 copy-start.3
  55.8 0.0 copy-start.4
  55.8 8.9 %fusion.5 = f32[128,1024]{1,0:T(8,128)S(1)} fusion(bf16[8192,1024]{1,0:T(8,128)(2,1)} %param.8, bf16[128,8192]{1,0:T(8,128)(2,1)} %all-gather.2.cloned.1.call-done, f32[8192]{0:T(1024)} %param.7, f32[128]{0:T(128)S(1)} %add_rsqrt_fusion), kind=kOutput, calls=%fused_computation.8 | convolution fusion | flops 2151677952 | bytes 19431936 | tf_op jit(solution)/shard_map/dot_general | solution.py:29
  64.8 0.0 copy-done
  64.8 2.8 %copy-done.3 = bf16[8192,1024]{1,0:T(8,128)(2,1)S(1)} copy-done((bf16[8192,1024]{1,0:T(8,128)(2,1)S(1)}, bf16[8192,1024]{1,0:T(8,128)(2,1)}, u32[]{:S(2)}) %copy-start.3) | copy-done | bytes 16777240
  67.6 0.0 copy-done.4
  67.6 2.5 %convolution_multiply_fusion = f32[128,1024]{1,0:T(8,128)S(1)} fusion(bf16[8192,1024]{1,0:T(8,128)(2,1)S(1)} %copy-done.3, bf16[128,8192]{1,0:T(8,128)(2,1)S(1)} %copy-done, f32[8192]{0:T(1024)S(1)} %copy-done.4, f32[128]{0:T(128)S(1)} %add_rsqrt_fusion, f32[128,1024]{1,0:T(8,128)S(1)} %fusion.5), kind=kOutput, calls=%fused_computation.5 | convolution fusion | flops 2152333312 | bytes 19956224 | tf_op jit(solution)/shard_map/dot_general | solution.py:30
  70.1 0.0 copy-start.2
  70.1 0.9 fusion.7
  71.0 0.3 copy.13
  71.4 17.5 %all_to_all.27 = f32[128,4,256]{2,1,0:T(4,128)S(1)} all-to-all(f32[128,4,256]{2,1,0:T(4,128)S(1)} %copy.13), channel_id=1, replica_groups=mesh['groups'=2,'hid'=16] {'hid'}, dimensions={0} | all-to-all | bytes 1048576 | tf_op jit(solution)/shard_map/all_to_all | solution.py:36
  88.9 0.2 all_to_all.23
  89.1 0.6 fusion.3
  89.7 0.8 copy.15
  90.6 4.2 %all-to-all-start.1 = ((bf16[8,64,256]{2,0,1:T(8,128)(2,1)}), bf16[8,64,256]{2,0,1:T(8,128)(2,1)S(1)}, u32[]{:S(2)}, u32[]{:S(2)}) async-start(bf16[8,64,256]{2,0,1:T(8,128)(2,1)} %copy.15), calls=%async_computation.1 | async-start | bytes 524288 | tf_op jit(solution)/shard_map/all_to_all | solution.py:39
  94.7 0.0 reduce-scatter.2.cloned.1.call-start
  94.8 0.0 copy-done.2
  94.8 9.9 %all-to-all-done.1 = bf16[8,64,256]{2,0,1:T(8,128)(2,1)S(1)} async-done(((bf16[8,64,256]{2,0,1:T(8,128)(2,1)}), bf16[8,64,256]{2,0,1:T(8,128)(2,1)S(1)}, u32[]{:S(2)}, u32[]{:S(2)}) %all-to-all-start.1) | async-done | bytes 262176 | tf_op jit(solution)/shard_map/all_to_all | solution.py:39
  104.8 0.1 copy.25
  105.0 10.1 %fusion.12 = f32[128,8192]{1,0:T(8,128)} fusion(bf16[1024,8192]{1,0:T(8,128)(2,1)} %param.10, bf16[128,1024]{1,0:T(8,128)(2,1)S(1)} %bitcast.29, bf16[1024]{0:T(1024)(128)(2,1)S(1)} %get-tuple-element.6, bf16[1024]{0:T(1024)(128)(2,1)S(1)} %get-tuple-element.5), kind=kOutput, calls=%fused_computation.21 | convolution fusion | flops 2147745792 | bytes 21237760 | tf_op jit(solution)/shard_map/dot_general | solution.py:46
  115.0 0.0 copy-start.1
  115.0 0.0 reduce-scatter.2.cloned.1.call-update
  115.1 71.2 %reduce-scatter.2.cloned.1.call-done = f32[8,8192]{1,0:T(8,128)} async-done(((f32[128,8192]{1,0:T(8,128)}), f32[8,8192]{1,0:T(8,128)}) %reduce-scatter.2.cloned.1.call-update) | async-done | bytes 262160 | tf_op jit(solution)/shard_map/reduce_scatter | solution.py:45
  186.2 0.0 copy-done.1
  186.2 1.6 add_convert_fusion
  (5 shorter events, 0.1 us)
Async XLA Ops:
  6.5 47.2 %all-gather.2.cloned.1.call-start = ((), (), s32[]{:S(2)}) async-start(), calls=%async_computation.3 | async-start | bytes 2228224 | tf_op jit(solution)/shard_map/all_gather | solution.py:27
  55.8 9.0 %copy-start = (bf16[128,8192]{1,0:T(8,128)(2,1)S(1)}, bf16[128,8192]{1,0:T(8,128)(2,1)}, u32[]{:S(2)}) copy-start(bf16[128,8192]{1,0:T(8,128)(2,1)} %all-gather.2.cloned.1.call-done) | copy-start | bytes 6291460
  55.8 11.8 %copy-start.3 = (bf16[8192,1024]{1,0:T(8,128)(2,1)S(1)}, bf16[8192,1024]{1,0:T(8,128)(2,1)}, u32[]{:S(2)}) copy-start(bf16[8192,1024]{1,0:T(8,128)(2,1)} %param.9) | copy-start | bytes 50331652
  55.8 11.8 %copy-start.4 = (f32[8192]{0:T(1024)S(1)}, f32[8192]{0:T(1024)}, u32[]{:S(2)}) copy-start(f32[8192]{0:T(1024)} %param.7) | copy-start | bytes 98308
  70.1 24.7 %copy-start.2 = (f32[1024]{0:T(1024)S(1)}, f32[1024]{0:T(1024)}, u32[]{:S(2)}) copy-start(f32[1024]{0:T(1024)} %param.11) | copy-start | bytes 12292
  90.6 14.2 %all-to-all-start.1 = ((bf16[8,64,256]{2,0,1:T(8,128)(2,1)}), bf16[8,64,256]{2,0,1:T(8,128)(2,1)S(1)}, u32[]{:S(2)}, u32[]{:S(2)}) async-start(bf16[8,64,256]{2,0,1:T(8,128)(2,1)} %copy.15), calls=%async_computation.1 | async-start | bytes 524288 | tf_op jit(solution)/shard_map/all_to_all | solution.py:39
  94.7 91.5 %reduce-scatter.2.cloned.1.call-start = ((), (), s32[]{:S(2)}) async-start(), calls=%async_computation.4 | async-start | bytes 4456448 | tf_op jit(solution)/shard_map/reduce_scatter | solution.py:45
  115.0 71.2 %copy-start.1 = (bf16[8,8192]{1,0:T(8,128)(2,1)S(1)}, bf16[8,8192]{1,0:T(8,128)(2,1)}, u32[]{:S(2)}) copy-start(bf16[8,8192]{1,0:T(8,128)(2,1)} %param.6) | copy-start | bytes 393220
Sparse Core Ops, SparseCore 0:
  9.5 44.1 all-gather.1
  115.2 70.9 reduce-scatter.1
where the time goes:
time: 195 us
  waiting for transfers between devices  128 us (66%)
  matrix products  23 us (12%)
  blocking collectives  17.5 us (9%)
  between operations  13.5 us (7%)
  local copies, waits for them, and re-layouts  4.41 us (2%)
  starting transfers between devices  4.21 us (2%)
  other arithmetic  3.77 us (2%)
    reduce_scatter x1, waiting for transfers between devices, shards(): lax.psum_scatter(jnp.dot(clipped, down_weight, preferred_element_type=jnp...  71.2 us
    all_gather x1, waiting for transfers between devices, shards(): whole = lax.all_gather(tokens, 'hid', axis=0, tiled=True)  46.5 us
    all_to_all x1, blocking collectives, shards(): lax.all_to_all(shaped, 'hid', split_axis=0, concat_axis=1, tiled=True)  17.5 us
    dot_general x1, matrix products, shards(): jnp.dot(clipped, down_weight, preferred_element_type=jnp.float32)  10.1 us
    all_to_all x1, waiting for transfers between devices, shards(): lax.all_to_all(turned.astype(jnp.bfloat16), 'hid', split_axis=1, concat_a...  9.94 us
    dot_general x1, matrix products, shards(): gate = jnp.dot(normed, gate_weight, preferred_element_type=jnp.float32)  8.95 us
    all_to_all x1, starting transfers between devices, shards(): lax.all_to_all(turned.astype(jnp.bfloat16), 'hid', split_axis=1, concat_a...  4.16 us
  transfers between devices with their start and end apart: 3, of which 3 were waited for; matrix products, arithmetic and copies ran while one was open for 0% of the time, Pallas kernels for 0%

commit v1 on v0

v1 whole, which is shorter than its diff:
```python
import functools
import math

import jax
import jax.numpy as jnp
from jax import lax
from jax.experimental import pallas as pl
from jax.experimental.pallas import tpu as pltpu
from jax.sharding import PartitionSpec as P

BLOCK = 256
STEPS = 4
TILE = 256
MESH = pl.DeviceIdType.MESH
BF = jnp.bfloat16
F32 = jnp.float32


def walsh(parts):
    parts = list(parts)
    half = 1
    while half < len(parts):
        for at in range(len(parts)):
            if at & half == 0:
                low, high = parts[at], parts[at + half]
                parts[at], parts[at + half] = low + high, low - high
        half *= 2
    return parts


def kernel(n, tok, gain, wg, wu, wd, clip, out,
           pair, x, vg, vu, vd, gate, up, table, hs, hr, bs, br, y,
           cs, cr, own, ys, yr, zs, zr, fs, fr, fk,
           wsem, dsem, pair_sem, ag_send, z_recv, y_recv, c_recv,
           a_send, a_recv, rs_send, rc_recv, ry_recv, rz_recv, rf_recv):
    me = lax.axis_index("hid")
    line = n // 4
    a, b, c = me // 4, (me // 2) % 2, me % 2
    rows, width = tok.shape
    both = 2 * rows
    local = vg.shape[1]
    total = n * rows
    span = width // STEPS
    piece = span // 2
    outs = out.shape[1]
    ospan = outs // STEPS
    opiece = ospan // 2
    core_peer = me + 1 - 2 * c
    y_peer = (a * 2 + 1 - b) * 2 + c

    def at_line(shift):
        return lax.rem(a + shift, line)

    def device(a_at):
        return (a_at * 2 + b) * 2 + c

    def strip(a_at, b_at):
        return pl.ds(pl.multiple_of((a_at * 2 + b_at) * both, both), both)

    def send(src, dst, ssem, rsem, to):
        pltpu.make_async_remote_copy(
            src_ref=src, dst_ref=dst, send_sem=ssem, recv_sem=rsem,
            device_id={"hid": to}, device_id_type=MESH).start()

    def settle(ref, sem):
        pltpu.make_async_copy(ref, ref, sem).wait()

    weight_copies = []
    for s in range(STEPS):
        part = pl.ds(s * span, span)
        weight_copies.append((
            pltpu.make_async_copy(wg.at[part, :], vg.at[part, :], wsem.at[0, s]),
            pltpu.make_async_copy(wu.at[part, :], vu.at[part, :], wsem.at[1, s])))
        for copy in weight_copies[-1]:
            copy.start()
    down_copies = []
    for t in range(STEPS):
        part = pl.ds(t * ospan, ospan)
        down_copies.append(pltpu.make_async_copy(wd.at[:, part], vd.at[:, part], dsem.at[t]))
        down_copies[-1].start()

    barrier = pltpu.get_barrier_semaphore()
    for shift in range(1, n):
        pl.semaphore_signal(barrier, inc=1, device_id={"hid": lax.rem(me + shift, n)}, device_id_type=MESH)
    pl.semaphore_wait(barrier, n - 1)

    send(tok, pair, pair_sem.at[0], pair_sem.at[1], core_peer)
    at_row = lax.broadcasted_iota(jnp.int32, (BLOCK, BLOCK), 0)
    at_col = lax.broadcasted_iota(jnp.int32, (BLOCK, BLOCK), 1)
    bits = at_row & at_col
    folded = bits
    for place in range(1, (BLOCK - 1).bit_length()):
        folded = folded ^ (bits >> place)
    table[...] = (1 - 2 * (folded & 1)).astype(F32).astype(BF)

    def normalized(ref):
        values = ref[...].astype(F32)
        inverse = lax.rsqrt(jnp.mean(values * values, axis=-1, keepdims=True) + 1e-05)
        return values * inverse * gain[...]

    mine = normalized(tok)
    settle(pair, pair_sem.at[1])
    other = normalized(pair)
    first = c == 0
    x[strip(a, b), :] = jnp.concatenate(
        [jnp.where(first, mine, other), jnp.where(first, other, mine)], axis=0).astype(BF)

    def cols(s, half):
        return pl.ds(pl.multiple_of(s * span + half * piece, piece), piece)

    for s in range(STEPS):
        block = x.at[strip(a, b), cols(s, c)]
        send(block, block, ag_send, y_recv.at[s, 0], y_peer)
        for shift in range(1, line):
            send(block, block, ag_send, z_recv.at[s, shift], device(at_line(shift)))

    def relay(s):
        for shift in range(1, line):
            block = x.at[strip(at_line(line - shift), b), cols(s, c)]
            settle(block, z_recv.at[s, shift])
            send(block, block, ag_send, y_recv.at[s, shift], y_peer)
            send(block, block, ag_send, c_recv.at[s], core_peer)
        for shift in range(line):
            block = x.at[strip(at_line(line - shift), 1 - b), cols(s, c)]
            settle(block, y_recv.at[s, shift])
            send(block, block, ag_send, c_recv.at[s], core_peer)

    def project(s):
        settle(x.at[pl.ds(0, total - both), cols(s, 1 - c)], c_recv.at[s])
        for copy in weight_copies[s]:
            copy.wait()
        part = pl.ds(s * span, span)

        @pl.loop(0, local // TILE)
        def _(j):
            tile = pl.ds(pl.multiple_of(j * TILE, TILE), TILE)
            for acc, weight in ((gate, vg), (up, vu)):
                term = jnp.dot(x[:, part], weight[part, tile], preferred_element_type=F32)
                acc[:, tile] = term if s == 0 else acc[:, tile] + term

    relay(0)
    for s in range(STEPS):
        if s + 1 < STEPS:
            relay(s + 1)
        project(s)

    blocks = []
    for at in range(local // BLOCK):
        tile = pl.ds(at * BLOCK, BLOCK)
        value = gate[:, tile]
        hidden = value / (1.0 + jnp.exp(-value)) * up[:, tile]
        gate[:, tile] = jnp.dot(hidden.astype(BF), table[...], preferred_element_type=F32)
    half = local // 2
    for d in range(n):
        part = pl.ds(d * rows, rows)
        values = gate[part, :]
        turned = walsh([values[:, at * BLOCK:(at + 1) * BLOCK] for at in range(local // BLOCK)])
        values = turned[0] if len(turned) == 1 else jnp.concatenate(turned, axis=1)
        hs[d] = jnp.concatenate([values[:, :half], values[:, half:]], axis=0).astype(BF)

    def exchange(src, dst, at):
        for shift in range(1, n):
            to = lax.rem(me + shift, n)
            send(src.at[to], dst.at[me], a_send.at[at], a_recv.at[at], to)
        dst[me] = src[me]
        settle(dst.at[pl.ds(0, n - 1)], a_recv.at[at])

    exchange(hs, hr, 0)
    factor = 1.0 / math.sqrt(n * local)
    lanes = 128
    for j in range(half // lanes):
        tile = pl.ds(j * lanes, lanes)
        turned = walsh([hr[d, :, tile].astype(F32) for d in range(n)])
        for d in range(n):
            bs[d, :, tile] = (turned[d] * factor).astype(BF)
    exchange(bs, br, 1)

    limit = 127.0 * clip[...]
    for q in range(n // 2):
        pieces = []
        for d in (2 * q, 2 * q + 1):
            values = br[d].astype(F32)
            pieces.append(jnp.concatenate([values[:rows], values[rows:]], axis=1))
        values = jnp.concatenate(pieces, axis=0)
        y[pl.ds(q * both, both), :] = jnp.clip(values, -limit, limit).astype(BF)

    def product(t, half_at, j):
        tile = pl.ds(pl.multiple_of(t * ospan + half_at * opiece + j * TILE, TILE), TILE)
        return jnp.dot(y[...], vd[:, tile], preferred_element_type=F32)

    def down(t):
        down_copies[t].wait()

        @pl.loop(0, opiece // TILE)
        def _(j):
            cs[t, :, pl.ds(pl.multiple_of(j * TILE, TILE), TILE)] = product(t, 1 - c, j).astype(BF)

        send(cs.at[t], cr.at[t], rs_send.at[0], rc_recv.at[t], core_peer)

        @pl.loop(0, opiece // TILE)
        def _(j):
            own[t, :, pl.ds(pl.multiple_of(j * TILE, TILE), TILE)] = product(t, c, j)

    def over_rows(t):
        settle(cr.at[t], rc_recv.at[t])
        for to in range(line):
            part = strip(to, 1 - b)
            ys[t, pl.ds(to * both, both), :] = (own[t, part, :] + cr[t, part, :].astype(F32)).astype(BF)
        send(ys.at[t], yr.at[t], rs_send.at[1], ry_recv.at[t], y_peer)

    def column_sum(t, a_at):
        part = strip(a_at, b)
        landed = yr[t, pl.ds(pl.multiple_of(a_at * both, both), both), :]
        return own[t, part, :] + cr[t, part, :].astype(F32) + landed.astype(F32)

    def over_line(t):
        settle(yr.at[t], ry_recv.at[t])
        for shift in range(1, line):
            zs[t, shift] = column_sum(t, at_line(shift)).astype(BF)
        for shift in range(1, line):
            send(zs.at[t, shift], zr.at[t, shift], rs_send.at[2], rz_recv.at[t], device(at_line(shift)))

    def finish(t):
        settle(zr.at[t, pl.ds(1, line - 1)], rz_recv.at[t])
        values = column_sum(t, a)
        for shift in range(1, line):
            values = values + zr[t, shift].astype(F32)
        fs[t] = jnp.where(first, values[rows:], values[:rows])
        fk[t] = jnp.where(first, values[:rows], values[rows:])
        send(fs.at[t], fr.at[t], rs_send.at[3], rf_recv.at[t], core_peer)

    for t in range(STEPS + 3):
        if t < STEPS:
            down(t)
        if 0 <= t - 1 < STEPS:
            over_rows(t - 1)
        if 0 <= t - 2 < STEPS:
            over_line(t - 2)
        if 0 <= t - 3 < STEPS:
            finish(t - 3)
    for t in range(STEPS):
        settle(fr.at[t], rf_recv.at[t])
        for half_at, sums in ((c, fk), (1 - c, fr)):
            part = pl.ds(pl.multiple_of(t * ospan + half_at * opiece, opiece), opiece)
            out[:, part] = (tok[:, part].astype(F32) + sums[t]).astype(out.dtype)

    settle(tok, pair_sem.at[0])
    settle(x.at[pl.ds(0, total - both), :], ag_send)
    settle(hs.at[pl.ds(0, n - 1)], a_send.at[0])
    settle(bs.at[pl.ds(0, n - 1)], a_send.at[1])
    settle(cs, rs_send.at[0])
    settle(ys, rs_send.at[1])
    settle(zs.at[:, pl.ds(1, line - 1)], rs_send.at[2])
    settle(fs, rs_send.at[3])


def layer(n, tokens, norm_gain, gate_weight, up_weight, down_weight, clip_scale):
    rows, width = tokens.shape
    local = gate_weight.shape[1]
    outs = down_weight.shape[1]
    total, both, line = n * rows, 2 * rows, n // 4
    opiece = outs // STEPS // 2
    vmem = pl.BlockSpec(memory_space=pltpu.VMEM)
    hbm = pl.BlockSpec(memory_space=pl.ANY)
    dma = pltpu.SemaphoreType.DMA
    swap = pltpu.VMEM((n, both, local // 2), BF)
    return pl.pallas_call(
        functools.partial(kernel, n),
        out_shape=jax.ShapeDtypeStruct((rows, outs), BF),
        in_specs=[vmem, vmem, hbm, hbm, hbm, vmem],
        out_specs=vmem,
        scratch_shapes=[
            pltpu.VMEM((rows, width), BF),
            pltpu.VMEM((total, width), BF),
            pltpu.VMEM((width, local), BF),
            pltpu.VMEM((width, local), BF),
            pltpu.VMEM((local, outs), BF),
            pltpu.VMEM((total, local), F32),
            pltpu.VMEM((total, local), F32),
            pltpu.VMEM((BLOCK, BLOCK), BF),
            swap, swap, swap, swap,
            pltpu.VMEM((total, local), BF),
            pltpu.VMEM((STEPS, total, opiece), BF),
            pltpu.VMEM((STEPS, total, opiece), BF),
            pltpu.VMEM((STEPS, total, opiece), F32),
            pltpu.VMEM((STEPS, line * both, opiece), BF),
            pltpu.VMEM((STEPS, line * both, opiece), BF),
            pltpu.VMEM((STEPS, line, both, opiece), BF),
            pltpu.VMEM((STEPS, line, both, opiece), BF),
            pltpu.VMEM((STEPS, rows, opiece), F32),
            pltpu.VMEM((STEPS, rows, opiece), F32),
            pltpu.VMEM((STEPS, rows, opiece), F32),
            dma((2, STEPS)), dma((STEPS,)), dma((2,)), dma(()),
            dma((STEPS, line)), dma((STEPS, line)), dma((STEPS,)),
            dma((2,)), dma((2,)), dma((4,)),
            dma((STEPS,)), dma((STEPS,)), dma((STEPS,)), dma((STEPS,)),
        ],
        compiler_params=pltpu.CompilerParams(
            collective_id=0, has_side_effects=True, vmem_limit_bytes=67043328),
    )(tokens, norm_gain.reshape(1, -1), gate_weight, up_weight, down_weight, clip_scale.reshape(1, -1))


def solution(mesh):
    in_specs = (
        P(("groups", "hid"), None),
        P(),
        P(None, "hid"),
        P(None, "hid"),
        P("hid", None),
        P("hid"),
    )
    return jax.shard_map(
        functools.partial(layer, mesh.shape["hid"]), mesh=mesh, in_specs=in_specs,
        out_specs=P(("groups", "hid"), None), check_vma=False)
```

time: 195 us -> 77.7 us (0.40)
  waiting for transfers between devices: 128 us -> 0 us
  Pallas kernels: 0 us -> 76 us
  matrix products: 23 us -> 0 us
  blocking collectives: 17.5 us -> 0 us
  between operations: 13.5 us -> 0.01 us
  starting transfers between devices: 4.21 us -> 0 us
  other arithmetic: 3.77 us -> 0 us
  local copies, waits for them, and re-layouts: 4.41 us -> 1.57 us
    pallas_call x0 -> x1, Pallas kernels: none -> 76 us  [layer(): pl.pallas_call(functools.partial(kernel, n), out_shape=jax.ShapeDtypeStru...]
    reduce_scatter x1 -> x0, waiting for transfers between devices: 71.2 us -> none  [shards(): lax.psum_scatter(jnp.dot(clipped, down_weight, preferred_element_type=jnp...]
    all_gather x1 -> x0, waiting for transfers between devices: 46.5 us -> none  [shards(): whole = lax.all_gather(tokens, 'hid', axis=0, tiled=True)]
    dot_general x5 -> x0, matrix products: 23 us -> none  [the longest x1 10.1 us: shards(): jnp.dot(clipped, down_weight, preferred_element_type=jnp.float32)]
    all_to_all x1 -> x0, blocking collectives: 17.5 us -> none  [shards(): lax.all_to_all(shaped, 'hid', split_axis=0, concat_axis=1, tiled=True)]
    all_to_all x1 -> x0, waiting for transfers between devices: 9.94 us -> none  [shards(): lax.all_to_all(turned.astype(jnp.bfloat16), 'hid', split_axis=1, concat_a...]
    all_to_all x1 -> x0, starting transfers between devices: 4.16 us -> none  [shards(): lax.all_to_all(turned.astype(jnp.bfloat16), 'hid', split_axis=1, concat_a...]
    reduce_sum x1 -> x0, other arithmetic: 2.08 us -> none  [normalize(): jnp.mean(values * values, axis=-1, keepdims=True) + 1e-05]
  transfers between devices with their start and end apart: 3 -> 0, of which waited for: 3 -> 0; matrix products, arithmetic and copies ran while one was open for 0% -> 0% of each run, Pallas kernels for 0% -> 0%
where the time goes in v1:
time: 77.7 us; the launch traced here: 77.6 us
  Pallas kernels  76 us (98%)
  local copies, waits for them, and re-layouts  1.57 us (2%)
    pallas_call x1, Pallas kernels, layer(): pl.pallas_call(functools.partial(kernel, n), out_shape=jax.ShapeDtypeStru...  76 us
    unnamed x1, local copies, waits for them, and re-layouts  1.57 us

profile of v1, /device:TPU:0, one launch (start us, length us, event | category | flops | bytes accessed | tf_op | source)
XLA Modules:
  0.0 77.6 jit_solution(7371135939958726335)
XLA Ops:
  0.0 76.0 %shard_map.64 = bf16[8,8192]{1,0:T(8,128)(2,1)} custom-call(bf16[8,8192]{1,0:T(8,128)(2,1)} %tok.1, f32[1,8192]{1,0:T(1,128)} %bitcast.2, bf16[8192,1024]{1,0:T(8,128)(2,1)} %wg.1, bf16[8192,1024]{1,0:T(8,128)(2,1)} %wu.1, bf16[1024,8192]{1,0:T(8,128)(2,1)} %wd.1, f32[1,1024]{1,0:T(1,128)} %bitcast.3), custom_call_target="tpu_custom_call" | custom-call | tf_op jit(solution)/shard_map/pallas_call | solution.py:267
  76.0 1.6 %copy.8 = bf16[8,8192]{1,0:T(8,128)(2,1)} copy(bf16[8,8192]{1,0:T(8,128)(2,1)} %shard_map.64) | data formatting | bytes 262144

commit v2 on v1

--- a/solution.py
+++ b/solution.py
@@ -10,6 +10,8 @@
 
 BLOCK = 256
 STEPS = 4
+OUT_STEPS = 8
+LAG = (1, 4, 7)
 TILE = 256
 MESH = pl.DeviceIdType.MESH
 BF = jnp.bfloat16
@@ -43,7 +45,7 @@
     span = width // STEPS
     piece = span // 2
     outs = out.shape[1]
-    ospan = outs // STEPS
+    ospan = outs // OUT_STEPS
     opiece = ospan // 2
     core_peer = me + 1 - 2 * c
     y_peer = (a * 2 + 1 - b) * 2 + c
@@ -74,7 +76,7 @@
         for copy in weight_copies[-1]:
             copy.start()
     down_copies = []
-    for t in range(STEPS):
+    for t in range(OUT_STEPS):
         part = pl.ds(t * ospan, ospan)
         down_copies.append(pltpu.make_async_copy(wd.at[:, part], vd.at[:, part], dsem.at[t]))
         down_copies[-1].start()
@@ -114,12 +116,14 @@
         for shift in range(1, line):
             send(block, block, ag_send, z_recv.at[s, shift], device(at_line(shift)))
 
-    def relay(s):
+    def relay_over(s):
         for shift in range(1, line):
             block = x.at[strip(at_line(line - shift), b), cols(s, c)]
             settle(block, z_recv.at[s, shift])
             send(block, block, ag_send, y_recv.at[s, shift], y_peer)
             send(block, block, ag_send, c_recv.at[s], core_peer)
+
+    def relay_core(s):
         for shift in range(line):
             block = x.at[strip(at_line(line - shift), 1 - b), cols(s, c)]
             settle(block, y_recv.at[s, shift])
@@ -138,11 +142,13 @@
                 term = jnp.dot(x[:, part], weight[part, tile], preferred_element_type=F32)
                 acc[:, tile] = term if s == 0 else acc[:, tile] + term
 
-    relay(0)
-    for s in range(STEPS):
-        if s + 1 < STEPS:
-            relay(s + 1)
-        project(s)
+    for s in range(STEPS + 2):
+        if s < STEPS:
+            relay_over(s)
+        if 0 <= s - 1 < STEPS:
+            relay_core(s - 1)
+        if 0 <= s - 2 < STEPS:
+            project(s - 2)
 
     blocks = []
     for at in range(local // BLOCK):
@@ -229,16 +235,12 @@
         fk[t] = jnp.where(first, values[:rows], values[rows:])
         send(fs.at[t], fr.at[t], rs_send.at[3], rf_recv.at[t], core_peer)
 
-    for t in range(STEPS + 3):
-        if t < STEPS:
-            down(t)
-        if 0 <= t - 1 < STEPS:
-            over_rows(t - 1)
-        if 0 <= t - 2 < STEPS:
-            over_line(t - 2)
-        if 0 <= t - 3 < STEPS:
-            finish(t - 3)
-    for t in range(STEPS):
+    stages = ((0, down), (LAG[0], over_rows), (LAG[1], over_line), (LAG[2], finish))
+    for t in range(OUT_STEPS + LAG[2]):
+        for lag, stage in stages:
+            if 0 <= t - lag < OUT_STEPS:
+                stage(t - lag)
+    for t in range(OUT_STEPS):
         settle(fr.at[t], rf_recv.at[t])
         for half_at, sums in ((c, fk), (1 - c, fr)):
             part = pl.ds(pl.multiple_of(t * ospan + half_at * opiece, opiece), opiece)
@@ -259,7 +261,7 @@
     local = gate_weight.shape[1]
     outs = down_weight.shape[1]
     total, both, line = n * rows, 2 * rows, n // 4
-    opiece = outs // STEPS // 2
+    opiece = outs // OUT_STEPS // 2
     vmem = pl.BlockSpec(memory_space=pltpu.VMEM)
     hbm = pl.BlockSpec(memory_space=pl.ANY)
     dma = pltpu.SemaphoreType.DMA
@@ -280,20 +282,20 @@
             pltpu.VMEM((BLOCK, BLOCK), BF),
             swap, swap, swap, swap,
             pltpu.VMEM((total, local), BF),
-            pltpu.VMEM((STEPS, total, opiece), BF),
-            pltpu.VMEM((STEPS, total, opiece), BF),
-            pltpu.VMEM((STEPS, total, opiece), F32),
-            pltpu.VMEM((STEPS, line * both, opiece), BF),
-            pltpu.VMEM((STEPS, line * both, opiece), BF),
-            pltpu.VMEM((STEPS, line, both, opiece), BF),
-            pltpu.VMEM((STEPS, line, both, opiece), BF),
-            pltpu.VMEM((STEPS, rows, opiece), F32),
-            pltpu.VMEM((STEPS, rows, opiece), F32),
-            pltpu.VMEM((STEPS, rows, opiece), F32),
-            dma((2, STEPS)), dma((STEPS,)), dma((2,)), dma(()),
+            pltpu.VMEM((OUT_STEPS, total, opiece), BF),
+            pltpu.VMEM((OUT_STEPS, total, opiece), BF),
+            pltpu.VMEM((OUT_STEPS, total, opiece), F32),
+            pltpu.VMEM((OUT_STEPS, line * both, opiece), BF),
+            pltpu.VMEM((OUT_STEPS, line * both, opiece), BF),
+            pltpu.VMEM((OUT_STEPS, line, both, opiece), BF),
+            pltpu.VMEM((OUT_STEPS, line, both, opiece), BF),
+            pltpu.VMEM((OUT_STEPS, rows, opiece), F32),
+            pltpu.VMEM((OUT_STEPS, rows, opiece), F32),
+            pltpu.VMEM((OUT_STEPS, rows, opiece), F32),
+            dma((2, STEPS)), dma((OUT_STEPS,)), dma((2,)), dma(()),
             dma((STEPS, line)), dma((STEPS, line)), dma((STEPS,)),
             dma((2,)), dma((2,)), dma((4,)),
-            dma((STEPS,)), dma((STEPS,)), dma((STEPS,)), dma((STEPS,)),
+            dma((OUT_STEPS,)), dma((OUT_STEPS,)), dma((OUT_STEPS,)), dma((OUT_STEPS,)),
         ],
         compiler_params=pltpu.CompilerParams(
             collective_id=0, has_side_effects=True, vmem_limit_bytes=67043328),

time: 77.7 us -> 68.3 us (0.88)
  Pallas kernels: 76 us -> 66.6 us
    pallas_call x1, Pallas kernels: 76 us -> 66.6 us  [layer(): pl.pallas_call(functools.partial(kernel, n), out_shape=jax.ShapeDtypeStru...]
where the time goes in v2:
time: 68.3 us; the launch traced here: 68.2 us
  Pallas kernels  66.6 us (98%)
  local copies, waits for them, and re-layouts  1.57 us (2%)
    pallas_call x1, Pallas kernels, layer(): pl.pallas_call(functools.partial(kernel, n), out_shape=jax.ShapeDtypeStru...  66.6 us
    unnamed x1, local copies, waits for them, and re-layouts  1.57 us

profile of v2, /device:TPU:0, one launch (start us, length us, event | category | flops | bytes accessed | tf_op | source)
XLA Modules:
  0.0 68.2 jit_solution(17063066195690502239)
XLA Ops:
  0.0 66.6 %shard_map.64 = bf16[8,8192]{1,0:T(8,128)(2,1)} custom-call(bf16[8,8192]{1,0:T(8,128)(2,1)} %tok.1, f32[1,8192]{1,0:T(1,128)} %bitcast.2, bf16[8192,1024]{1,0:T(8,128)(2,1)} %wg.1, bf16[8192,1024]{1,0:T(8,128)(2,1)} %wu.1, bf16[1024,8192]{1,0:T(8,128)(2,1)} %wd.1, f32[1,1024]{1,0:T(1,128)} %bitcast.3), custom_call_target="tpu_custom_call" | custom-call | tf_op jit(solution)/shard_map/pallas_call | solution.py:269
  66.6 1.6 %copy.8 = bf16[8,8192]{1,0:T(8,128)(2,1)} copy(bf16[8,8192]{1,0:T(8,128)(2,1)} %shard_map.64) | data formatting | bytes 262144
